TPU v7x, 32 devices: a whole 2x2x4 slice. The times are simulated.
32 devices in a mesh: groups: 2 (over x), seq: 16 (over z, y, core).
Axes of the slice: x: 2, y: 2, z: 4, core: 2. Of those that a mesh axis runs over, the one named last changes fastest.
Arguments:
- queries: bfloat16 [4096, 2048], P(('groups', 'seq')), parts along dimension 0, may hold values from -2.5 to 2.5
- keys: bfloat16 [4096, 2048], P(('groups', 'seq')), parts along dimension 0, may hold values from -2.5 to 2.5
- values: bfloat16 [4096, 2048], P(('groups', 'seq')), parts along dimension 0, may hold values from -6 to 6
- grad_out: bfloat16 [4096, 2048], P(('groups', 'seq')), parts along dimension 0, may hold values from -6 to 6
- doc_lengths: int32 [16], P('groups'), parts along dimension 0, may hold values from 1 to 896, 2048 in all
Outputs:
- attn_out: bfloat16 [4096, 2048], P(('groups', 'seq')), parts along dimension 0
- grad_queries: bfloat16 [4096, 2048], P(('groups', 'seq')), parts along dimension 0
- grad_keys: bfloat16 [4096, 2048], P(('groups', 'seq')), parts along dimension 0
- grad_values: bfloat16 [4096, 2048], P(('groups', 'seq')), parts along dimension 0
There are 2 independent parts, one for each index of `groups`. A program takes and returns all parts, laid end to end along the dimension named above; each array names one. Nothing has to cross between parts.
Inputs may be any that keep to these rules, and one draw needn't show every extreme that they name: `doc_lengths`: lengths of the documents in order; they sum to 2048 and the longest has exactly 896 tokens.
All inputs are finite; a program needn't handle non-finite values.
Results may differ from a plain program's by a relative error of at most 0.0058.
Values may be sent and summed in bfloat16 or wider, within the bound.
A program may use at most 256 MiB of HBM per device.

v0:
```python
import functools

import jax
import jax.numpy as jnp
from jax import lax
from jax.experimental import pallas as pl
from jax.experimental.pallas import tpu as pltpu
from jax.sharding import PartitionSpec as P

HD = 128
CHUNK = 2
MINOR, ACROSS, NEXT, SECOND, CARRY = range(5)

F32 = jnp.float32
BF16 = jnp.bfloat16


def dot(a, b, contract=(1, 0)):
    dims = (((contract[0],), (contract[1],)), ((), ()))
    return lax.dot_general(a, b, dims, preferred_element_type=F32)


def kernel(n, docs, heads, lengths_hbm, q_hbm, k_hbm, v_hbm, g_hbm, attn_hbm, gq_hbm, gk_hbm, gv_hbm,
           attn_ref, gq_ref, gk_ref, gv_ref, store_sems, lengths, q_ref, k_ref, v_ref, g_ref, load_sems, sg_ref, states, minor_in, sum_out, sum_in, total_out, next_in, second_in, carry_out,
           entering, weights_ref, dweights_ref, send_sems, recv_sems):
    loads = [pltpu.make_async_copy(src, dst, load_sems.at[i]) for i, (src, dst) in enumerate((
        (lengths_hbm, lengths), (g_hbm, g_ref), (q_hbm, q_ref), (k_hbm, k_ref), (v_hbm, v_ref)))]
    for load in loads:
        load.start()
    rows = q_ref.shape[0]
    planes = n // 4
    chunks = heads // CHUNK
    me = lax.axis_index("seq")
    core = lax.rem(me, 2)
    plane = me // 4
    chip = lax.rem(me // 2, 2)
    partner = me + 1 - 2 * core
    across = me + 2 - 4 * chip
    step = 2 * core - 1
    major, minor = 1 - core, core

    def inside(p):
        return (p >= 0) & (p < planes)

    barrier = pltpu.get_barrier_semaphore()

    def greet(device):
        pl.semaphore_signal(barrier, inc=1, device_id={"seq": device},
                            device_id_type=pl.DeviceIdType.MESH)

    greet(partner)
    greet(across)
    for by in (-1, 1):
        @pl.when(inside(plane + by))
        def _():
            greet(me + 4 * by)

    loads[0].wait()
    starts = []
    running = jnp.int32(0)
    for j in range(docs):
        starts.append(running)
        running = running + lengths[j]

    shift = 1 - core

    def clear(first, last):
        lower = first * rows + shift
        upper = (last + 1) * rows + shift
        found = jnp.int32(0)
        for s in starts:
            found = found + jnp.where((s >= lower) & (s < upper), 1, 0)
        return found == 0

    own_clear = clear(me, me)
    partner_clear = clear(partner, partner)
    is_down = chip == core
    down_first = 4 * plane + 2 * core
    up_first = 4 * plane + 2 - 2 * core
    down_clear = clear(down_first, down_first + 1)
    up_clear = clear(up_first, up_first + 1)
    before_first = 4 * (plane - step)
    before_clear = clear(before_first, before_first + 3)
    use_next = inside(plane - step) & (jnp.logical_not(is_down) | up_clear)
    use_second = use_next & before_clear & inside(plane - 2 * step)

    first_row = me * rows
    seq_total = rows * n

    def spans(shape, axis):
        pos = first_row + lax.broadcasted_iota(jnp.int32, shape, axis)
        begin = jnp.zeros(shape, jnp.int32)
        finish = jnp.full(shape, seq_total, jnp.int32)
        for s in starts:
            begin = jnp.where(s <= pos, s, begin)
        for s in reversed(starts):
            finish = jnp.where(s > pos, s, finish)
        return pos, begin, finish

    pos, begin, finish = spans((rows, HD), 0)
    pos_row, begin_row, _ = spans((rows, rows), 1)
    inv_root = 1.0 / jnp.sqrt((pos - begin + 1).astype(F32))
    pos_square, begin_square, _ = spans((rows, rows), 0)
    same_doc = (begin_square == begin_row) & (pos_row <= pos_square)
    tail_rows = jnp.where(finish >= first_row + rows, 1.0, 0.0).astype(BF16)
    head_rows = jnp.where(begin <= first_row, 1.0, 0.0).astype(BF16)
    prefix_rows = jnp.where(begin < first_row, 1.0, 0.0).astype(BF16)
    suffix_rows = jnp.where(finish > first_row + rows, 1.0, 0.0).astype(BF16)

    def columns(h):
        return pl.ds(pl.multiple_of(h * HD, HD), HD)

    def copy(kind, i, src, dst, device):
        return pltpu.make_async_remote_copy(
            src_ref=src, dst_ref=dst, send_sem=send_sems.at[kind, i],
            recv_sem=recv_sems.at[kind, i], device_id={"seq": device},
            device_id_type=pl.DeviceIdType.MESH)

    def part(i):
        return pl.ds(i * CHUNK, CHUNK)

    def minor_copy(i):
        return copy(MINOR, i, states.at[minor, part(i)], minor_in.at[part(i)], partner)

    def across_copy(i):
        return copy(ACROSS, i, sum_out.at[part(i)], sum_in.at[part(i)], across)

    def next_copy(i):
        return copy(NEXT, i, total_out.at[part(i)], next_in.at[part(i)], me + 4 * step)

    def second_copy(i):
        return copy(SECOND, i, next_in.at[part(i)], second_in.at[part(i)], me + 4 * step)

    def carry_copy(i):
        return copy(CARRY, i, carry_out.at[part(i)], entering.at[major, part(i)], partner)

    def own_states(i):
        for j in range(CHUNK):
            h = i * CHUNK + j
            at = columns(h)
            sg = (g_ref[:, at].astype(F32) * inv_root).astype(BF16)
            sg_ref[:, at] = sg
            states[0, h] = dot(k_ref[:, at] * tail_rows, v_ref[:, at], (0, 0)).astype(BF16)
            states[1, h] = dot(q_ref[:, at] * head_rows, sg, (0, 0)).astype(BF16)

    for load in loads[1:]:
        load.wait()
    own_states(0)
    peers = jnp.int32(2)
    for by in (-1, 1):
        peers = peers + jnp.where(inside(plane + by), 1, 0)
    pl.semaphore_wait(barrier, peers)
    minor_copy(0).start()


    def pick(flag, x):
        return jnp.where(flag, x.astype(F32), 0.0)

    def chip_sum(i):
        minor_copy(i).wait_recv()
        for j in range(CHUNK):
            h = i * CHUNK + j
            sum_out[h] = (states[major, h].astype(F32) + pick(own_clear, minor_in[h])).astype(BF16)
        across_copy(i).start()

    @pl.loop(1, chunks + 2)
    def _(i):
        @pl.when(i < chunks)
        def _():
            own_states(i)
            minor_copy(i).start()

        @pl.when(i >= 2)
        def _():
            chip_sum(i - 2)

    def total(i):
        for j in range(CHUNK):
            h = i * CHUNK + j
            at = columns(h)
            scores = dot(q_ref[:, at], k_ref[:, at], (1, 1))
            weights_ref[h] = jnp.where(same_doc, scores, 0.0).astype(BF16)
            dscores = dot(sg_ref[:, at], v_ref[:, at], (1, 1))
            dweights_ref[h] = jnp.where(same_doc, dscores, 0.0).astype(BF16)
        across_copy(i).wait_recv()
        for j in range(CHUNK):
            h = i * CHUNK + j
            total_out[h] = (pick(is_down | down_clear, sum_out[h])
                            + pick(jnp.logical_not(is_down) | down_clear, sum_in[h])).astype(BF16)

        @pl.when(inside(plane + step))
        def _():
            next_copy(i).start()

    relays = inside(plane - step) & inside(plane + step)

    def relay(i):
        @pl.when(inside(plane - step))
        def _():
            next_copy(i).wait_recv()

        @pl.when(relays)
        def _():
            second_copy(i).start()

    def enter(i):
        @pl.when(inside(plane - 2 * step))
        def _():
            second_copy(i).wait_recv()

        for j in range(CHUNK):
            h = i * CHUNK + j
            carry = pick(is_down, sum_in[h]) + pick(use_next, next_in[h]) + pick(use_second, second_in[h])
            carry_out[h] = carry.astype(BF16)
            entering[major, h] = (minor_in[h].astype(F32) + pick(partner_clear, carry)).astype(BF16)
        carry_copy(i).start()

    def stores(i):
        at = pl.ds(pl.multiple_of(i * CHUNK * HD, CHUNK * HD), CHUNK * HD)
        return [pltpu.make_async_copy(src.at[:, at], dst.at[:, at], store_sems.at[which, i])
                for which, (src, dst) in enumerate(((attn_ref, attn_hbm), (gq_ref, gq_hbm),
                                                    (gk_ref, gk_hbm), (gv_ref, gv_hbm)))]

    def finish_heads(i):
        carry_copy(i).wait_recv()
        for j in range(CHUNK):
            h = i * CHUNK + j
            at = columns(h)
            q, k, v, sg = q_ref[:, at], k_ref[:, at], v_ref[:, at], sg_ref[:, at]
            w, dw = weights_ref[h], dweights_ref[h]
            carried, returned = entering[0, h], entering[1, h]
            attended = dot(w, v) + dot(q * prefix_rows, carried)
            attn_ref[:, at] = (attended * inv_root).astype(BF16)
            gq_ref[:, at] = (dot(dw, k) + dot(sg * prefix_rows, carried, (1, 1))).astype(BF16)
            gk_ref[:, at] = (dot(dw, q, (0, 0)) + dot(v * suffix_rows, returned, (1, 1))).astype(BF16)
            gv_ref[:, at] = (dot(w, sg, (0, 0)) + dot(k * suffix_rows, returned)).astype(BF16)
        for store in stores(i):
            store.start()

    stages = ((0, total), (2, relay), (4, enter), (5, finish_heads))

    @pl.loop(0, chunks + stages[-1][0])
    def _(i):
        for lag, stage in stages:
            @pl.when((i >= lag) & (i < chunks + lag))
            def _():
                stage(i - lag)

    @pl.loop(0, chunks)
    def _(i):
        for store in stores(i):
            store.wait()
        minor_copy(i).wait_send()
        across_copy(i).wait_send()
        carry_copy(i).wait_send()

        @pl.when(inside(plane + step))
        def _():
            next_copy(i).wait_send()

        @pl.when(relays)
        def _():
            second_copy(i).wait_send()


def place(*refs):
    sources, targets, held, sems = refs[:4], refs[4:8], refs[8], refs[9]
    rows = sources[0].shape[0] // 2
    pieces = [(i, pl.ds(half * rows, rows), 4 * half + i) for half in range(2) for i in range(4)]
    inward = [pltpu.make_async_copy(sources[i].at[at], held.at[i, at], sems.at[0, s]) for i, at, s in pieces]
    outward = [pltpu.make_async_copy(held.at[i, at], targets[i].at[at], sems.at[1, s]) for i, at, s in pieces]
    for move in inward:
        move.start()
    for arrive, leave in zip(inward, outward):
        arrive.wait()
        leave.start()
    for move in outward:
        move.wait()


def per_device(n, queries, keys, values, grad_out, doc_lengths):
    rows, width = queries.shape
    heads = width // HD
    chunks = heads // CHUNK
    remote = pl.BlockSpec(memory_space=pltpu.HBM)
    held = pltpu.VMEM((rows, width), BF16)
    state = pltpu.VMEM((heads, HD, HD), BF16)
    pair = pltpu.VMEM((2, heads, HD, HD), BF16)
    square = pltpu.VMEM((heads, rows, rows), BF16)
    out = jax.ShapeDtypeStruct((rows, width), BF16)
    results = pl.pallas_call(
        functools.partial(kernel, n, doc_lengths.shape[0], heads),
        out_shape=(out,) * 4,
        in_specs=[remote] * 5,
        out_specs=(remote,) * 4,
        scratch_shapes=[held] * 4 + [pltpu.SemaphoreType.DMA((4, chunks)), pltpu.SMEM(doc_lengths.shape, jnp.int32)] + [held] * 4
        + [pltpu.SemaphoreType.DMA((5,)), held, pair] + [state] * 7 + [pair, square, square]
        + [pltpu.SemaphoreType.DMA((5, chunks))] * 2,
        compiler_params=pltpu.CompilerParams(
            collective_id=0, has_side_effects=True, vmem_limit_bytes=64_700_000),
    )(doc_lengths, queries, keys, values, grad_out)
    return pl.pallas_call(
        place,
        out_shape=(out,) * 4,
        in_specs=[remote] * 4,
        out_specs=(remote,) * 4,
        scratch_shapes=[pltpu.VMEM((4, rows, width), BF16), pltpu.SemaphoreType.DMA((2, 8))],
        compiler_params=pltpu.CompilerParams(vmem_limit_bytes=64_700_000),
    )(*results)


def solution(mesh):
    rows = P(("groups", "seq"), None)
    return jax.shard_map(
        functools.partial(per_device, mesh.shape["seq"]),
        mesh=mesh,
        in_specs=(rows, rows, rows, rows, P("groups")),
        out_specs=(rows,) * 4,
        check_vma=False,
    )
```

profile of v0, /device:TPU:1, one launch (start us, length us, event | category | flops | bytes accessed | tf_op | source)
XLA Modules:
  0.0 32.0 jit_solution(4283068929653942963)
XLA Ops:
  0.6 29.0 %shard_map.84 = (bf16[128,2048]{1,0:T(8,128)(2,1)}, bf16[128,2048]{1,0:T(8,128)(2,1)}, bf16[128,2048]{1,0:T(8,128)(2,1)}, bf16[128,2048]{1,0:T(8,128)(2,1)}) custom-call(s32[8]{0:T(128)} %lengths_hbm.1, bf16[128,2048]{1,0:T(8,128)(2,1)} %q_hbm.1, bf16[128,2048]{1,0:T(8,128)(2,1)} %k_hbm.1, bf16[128,2048]{1,0:T(8,128)(2,1)} %v_hbm.1, bf16[128,2048]{1,0:T(8,128)(2,1)} %g_hbm.1), custom_call_target="tpu_custom_call" | custom-call | tf_op jit(solution)/shard_map/pallas_call | solution.py:291
  29.6 2.4 %shard_map.85 = (bf16[128,2048]{1,0:T(8,128)(2,1)}, bf16[128,2048]{1,0:T(8,128)(2,1)}, bf16[128,2048]{1,0:T(8,128)(2,1)}, bf16[128,2048]{1,0:T(8,128)(2,1)}) custom-call(bf16[128,2048]{1,0:T(8,128)(2,1)} %get-tuple-element.8.refs_0_, bf16[128,2048]{1,0:T(8,128)(2,1)} %get-tuple-element.9.refs_1_, bf16[128,2048]{1,0:T(8,128)(2,1)} %get-tuple-element.10.refs_2_, ...), custom_call_target="tpu_custom_call" | custom-call | tf_op jit(solution)/shard_map/pallas_call | solution.py:302
where the time goes:
time: 32.2 us; the launch traced here: 32 us
  Pallas kernels  31.4 us (98%)
  between operations  0.64 us (2%)
    pallas_call x1, Pallas kernels, per_device(): pl.pallas_call(functools.partial(kernel, n, doc_lengths.shape[0], heads),...  29 us
    pallas_call x1, Pallas kernels, per_device(): pl.pallas_call(place, out_shape=(out,) * 4, in_specs=[remote] * 4, out_sp...  2.4 us

commit v1 on v0

--- a/solution.py
+++ b/solution.py
@@ -20,8 +20,8 @@
     return lax.dot_general(a, b, dims, preferred_element_type=F32)
 
 
-def kernel(n, docs, heads, lengths_hbm, q_hbm, k_hbm, v_hbm, g_hbm, attn_hbm, gq_hbm, gk_hbm, gv_hbm,
-           attn_ref, gq_ref, gk_ref, gv_ref, store_sems, lengths, q_ref, k_ref, v_ref, g_ref, load_sems, sg_ref, states, minor_in, sum_out, sum_in, total_out, next_in, second_in, carry_out,
+def kernel(n, docs, heads, lengths_hbm, q_hbm, k_hbm, v_hbm, g_hbm, attn_ref, gq_ref, gk_ref, gv_ref,
+           lengths, q_ref, k_ref, v_ref, g_ref, load_sems, sg_ref, states, minor_in, sum_out, sum_in, total_out, next_in, second_in, carry_out,
            entering, weights_ref, dweights_ref, send_sems, recv_sems):
     loads = [pltpu.make_async_copy(src, dst, load_sems.at[i]) for i, (src, dst) in enumerate((
         (lengths_hbm, lengths), (g_hbm, g_ref), (q_hbm, q_ref), (k_hbm, k_ref), (v_hbm, v_ref)))]
@@ -215,12 +215,6 @@
             entering[major, h] = (minor_in[h].astype(F32) + pick(partner_clear, carry)).astype(BF16)
         carry_copy(i).start()
 
-    def stores(i):
-        at = pl.ds(pl.multiple_of(i * CHUNK * HD, CHUNK * HD), CHUNK * HD)
-        return [pltpu.make_async_copy(src.at[:, at], dst.at[:, at], store_sems.at[which, i])
-                for which, (src, dst) in enumerate(((attn_ref, attn_hbm), (gq_ref, gq_hbm),
-                                                    (gk_ref, gk_hbm), (gv_ref, gv_hbm)))]
-
     def finish_heads(i):
         carry_copy(i).wait_recv()
         for j in range(CHUNK):
@@ -234,8 +228,6 @@
             gq_ref[:, at] = (dot(dw, k) + dot(sg * prefix_rows, carried, (1, 1))).astype(BF16)
             gk_ref[:, at] = (dot(dw, q, (0, 0)) + dot(v * suffix_rows, returned, (1, 1))).astype(BF16)
             gv_ref[:, at] = (dot(w, sg, (0, 0)) + dot(k * suffix_rows, returned)).astype(BF16)
-        for store in stores(i):
-            store.start()
 
     stages = ((0, total), (2, relay), (4, enter), (5, finish_heads))
 
@@ -248,8 +240,6 @@
 
     @pl.loop(0, chunks)
     def _(i):
-        for store in stores(i):
-            store.wait()
         minor_copy(i).wait_send()
         across_copy(i).wait_send()
         carry_copy(i).wait_send()
@@ -264,17 +254,11 @@
 
 
 def place(*refs):
-    sources, targets, held, sems = refs[:4], refs[4:8], refs[8], refs[9]
-    rows = sources[0].shape[0] // 2
-    pieces = [(i, pl.ds(half * rows, rows), 4 * half + i) for half in range(2) for i in range(4)]
-    inward = [pltpu.make_async_copy(sources[i].at[at], held.at[i, at], sems.at[0, s]) for i, at, s in pieces]
-    outward = [pltpu.make_async_copy(held.at[i, at], targets[i].at[at], sems.at[1, s]) for i, at, s in pieces]
-    for move in inward:
+    sources, targets, sems = refs[:4], refs[4:8], refs[8]
+    moves = [pltpu.make_async_copy(src, dst, sems.at[i]) for i, (src, dst) in enumerate(zip(sources, targets))]
+    for move in moves:
         move.start()
-    for arrive, leave in zip(inward, outward):
-        arrive.wait()
-        leave.start()
-    for move in outward:
+    for move in moves:
         move.wait()
 
 
@@ -290,22 +274,22 @@
     out = jax.ShapeDtypeStruct((rows, width), BF16)
     results = pl.pallas_call(
         functools.partial(kernel, n, doc_lengths.shape[0], heads),
-        out_shape=(out,) * 4,
+        out_shape=(held,) * 4,
         in_specs=[remote] * 5,
-        out_specs=(remote,) * 4,
-        scratch_shapes=[held] * 4 + [pltpu.SemaphoreType.DMA((4, chunks)), pltpu.SMEM(doc_lengths.shape, jnp.int32)] + [held] * 4
+        out_specs=(pl.BlockSpec(memory_space=pltpu.VMEM),) * 4,
+        scratch_shapes=[pltpu.SMEM(doc_lengths.shape, jnp.int32)] + [held] * 4
         + [pltpu.SemaphoreType.DMA((5,)), held, pair] + [state] * 7 + [pair, square, square]
         + [pltpu.SemaphoreType.DMA((5, chunks))] * 2,
         compiler_params=pltpu.CompilerParams(
-            collective_id=0, has_side_effects=True, vmem_limit_bytes=64_700_000),
+            collective_id=0, has_side_effects=True, vmem_limit_bytes=64946176),
     )(doc_lengths, queries, keys, values, grad_out)
     return pl.pallas_call(
         place,
         out_shape=(out,) * 4,
-        in_specs=[remote] * 4,
+        in_specs=[pl.BlockSpec(memory_space=pltpu.VMEM)] * 4,
         out_specs=(remote,) * 4,
-        scratch_shapes=[pltpu.VMEM((4, rows, width), BF16), pltpu.SemaphoreType.DMA((2, 8))],
-        compiler_params=pltpu.CompilerParams(vmem_limit_bytes=64_700_000),
+        scratch_shapes=[pltpu.SemaphoreType.DMA((4,))],
+        compiler_params=pltpu.CompilerParams(vmem_limit_bytes=16_000_000),
     )(*results)
 
 

time: 32.2 us -> 30.2 us (0.938)
  Pallas kernels: 31.4 us -> 29.4 us
    pallas_call x1, Pallas kernels: 2.4 us -> 1.35 us  [per_device(): pl.pallas_call(place, out_shape=(out,) * 4, in_specs=[pl.BlockSpec(memory...]
    pallas_call x1, Pallas kernels: 29 us -> 28.1 us  [per_device(): pl.pallas_call(functools.partial(kernel, n, doc_lengths.shape[0], heads),...]
where the time goes in v1:
time: 30.2 us; the launch traced here: 30.1 us
  Pallas kernels  29.4 us (97%)
  between operations  0.64 us (2%)
    pallas_call x1, Pallas kernels, per_device(): pl.pallas_call(functools.partial(kernel, n, doc_lengths.shape[0], heads),...  28.1 us
    pallas_call x1, Pallas kernels, per_device(): pl.pallas_call(place, out_shape=(out,) * 4, in_specs=[pl.BlockSpec(memory...  1.35 us

profile of v1, /device:TPU:1, one launch (start us, length us, event | category | flops | bytes accessed | tf_op | source)
XLA Modules:
  0.0 30.1 jit_solution(1183396071781287199)
XLA Ops:
  0.6 28.1 %shard_map.84 = (bf16[128,2048]{1,0:T(8,128)(2,1)S(1)}, bf16[128,2048]{1,0:T(8,128)(2,1)S(1)}, bf16[128,2048]{1,0:T(8,128)(2,1)S(1)}, bf16[128,2048]{1,0:T(8,128)(2,1)S(1)}) custom-call(s32[8]{0:T(128)} %lengths_hbm.1, bf16[128,2048]{1,0:T(8,128)(2,1)} %q_hbm.1, bf16[128,2048]{1,0:T(8,128)(2,1)} %k_hbm.1, bf16[128,2048]{1,0:T(8,128)(2,1)} %v_hbm.1, ...), custom_call_target="tpu_custom_call" | custom-call | tf_op jit(solution)/shard_map/pallas_call | solution.py:275
  28.7 1.3 %shard_map.85 = (bf16[128,2048]{1,0:T(8,128)(2,1)}, bf16[128,2048]{1,0:T(8,128)(2,1)}, bf16[128,2048]{1,0:T(8,128)(2,1)}, bf16[128,2048]{1,0:T(8,128)(2,1)}) custom-call(bf16[128,2048]{1,0:T(8,128)(2,1)S(1)} %get-tuple-element.8.refs_0_, bf16[128,2048]{1,0:T(8,128)(2,1)S(1)} %get-tuple-element.9.refs_1_, bf16[128,2048]{1,0:T(8,128)(2,1)S(1)} %get-tuple-element.10.refs_2_, ...), custom_call_target="tpu_custom_call" | custom-call | tf_op jit(solution)/shard_map/pallas_call | solution.py:286

commit v2 on v1

v2 whole, which is shorter than its diff:
```python
import functools

import jax
import jax.numpy as jnp
from jax import lax
from jax.experimental import pallas as pl
from jax.experimental.pallas import tpu as pltpu
from jax.sharding import PartitionSpec as P

HD = 128
CHUNK = 2
FORWARD, BACKWARD = 0, 1
MINOR, ACROSS, NEXT, SECOND, CARRY = range(5)
VMEM_BYTES = 67_043_328

F32 = jnp.float32
BF16 = jnp.bfloat16


def dot(a, b, contract=(1, 0)):
    dims = (((contract[0],), (contract[1],)), ((), ()))
    return lax.dot_general(a, b, dims, preferred_element_type=F32)


def pick(flag, x):
    return jnp.where(flag, x.astype(F32), 0.0)


def kernel(n, docs, heads, lengths_hbm, q_hbm, k_hbm, v_hbm, g_hbm, attn_ref, gq_ref, gk_ref, gv_ref,
           lengths, q_ref, k_ref, v_ref, g_ref, load_sems, sg_ref, states, minor_in, sum_out, sum_in,
           total_out, next_in, second_in, carry_out, entering, weights_ref, dweights_ref, send_sems, recv_sems):
    loads = [pltpu.make_async_copy(src, dst, load_sems.at[i]) for i, (src, dst) in enumerate((
        (lengths_hbm, lengths), (g_hbm, g_ref), (q_hbm, q_ref), (k_hbm, k_ref), (v_hbm, v_ref)))]
    for load in loads:
        load.start()
    rows = q_ref.shape[0]
    planes = n // 4
    chunks = heads // CHUNK
    me = lax.axis_index("seq")
    core = lax.rem(me, 2)
    plane = me // 4
    chip = lax.rem(me // 2, 2)
    partner = me + 1 - 2 * core
    across = me + 2 - 4 * chip
    step = 2 * core - 1
    major, minor = 1 - core, core

    def inside(p):
        return (p >= 0) & (p < planes)

    barrier = pltpu.get_barrier_semaphore()

    def greet(device):
        pl.semaphore_signal(barrier, inc=1, device_id={"seq": device},
                            device_id_type=pl.DeviceIdType.MESH)

    greet(partner)
    greet(across)
    for by in (-1, 1):
        @pl.when(inside(plane + by))
        def _():
            greet(me + 4 * by)

    loads[0].wait()
    starts = []
    running = jnp.int32(0)
    for j in range(docs):
        starts.append(running)
        running = running + lengths[j]

    def clear(d, first, last):
        lower = first * rows + d
        upper = (last + 1) * rows + d
        found = jnp.int32(0)
        for s in starts:
            found = found + jnp.where((s >= lower) & (s < upper), 1, 0)
        return found == 0

    own_clear = clear(major, me, me)
    partner_clear = clear(major, partner, partner)
    is_down = chip == core
    down_first = 4 * plane + 2 * core
    up_first = 4 * plane + 2 - 2 * core
    down_clear = clear(major, down_first, down_first + 1)
    up_clear = clear(major, up_first, up_first + 1)
    before_first = 4 * (plane - step)
    before_clear = clear(major, before_first, before_first + 3)
    plane_clear = down_clear & up_clear
    has_before = inside(plane - step)
    has_after = inside(plane + step)
    last = jnp.logical_not(inside(plane + 2 * step))
    merges = has_before & has_after & last & (core == 1)
    relays = has_before & has_after & jnp.logical_not(merges)
    has_second = (has_after | (core == 0)) & inside(plane - 2 * step)
    sends_across = jnp.logical_not(is_down) | has_after
    takes_across = is_down | has_after
    use_next = has_before & (jnp.logical_not(is_down) | up_clear)
    use_second = use_next & before_clear & has_second

    first_row = me * rows
    seq_total = rows * n

    def spans(shape, axis):
        pos = first_row + lax.broadcasted_iota(jnp.int32, shape, axis)
        begin = jnp.zeros(shape, jnp.int32)
        finish = jnp.full(shape, seq_total, jnp.int32)
        for s in starts:
            begin = jnp.where(s <= pos, s, begin)
        for s in reversed(starts):
            finish = jnp.where(s > pos, s, finish)
        return pos, begin, finish

    pos, begin, finish = spans((rows, HD), 0)
    inv_root = 1.0 / jnp.sqrt((pos - begin + 1).astype(F32))
    tail_rows = jnp.where(finish >= first_row + rows, 1.0, 0.0).astype(BF16)
    head_rows = jnp.where(begin <= first_row, 1.0, 0.0).astype(BF16)
    prefix_rows = jnp.where(begin < first_row, 1.0, 0.0).astype(BF16)
    suffix_rows = jnp.where(finish > first_row + rows, 1.0, 0.0).astype(BF16)
    pos_row, begin_row, _ = spans((1, rows), 1)
    pos_square, begin_square, _ = spans((rows, rows), 0)
    same_doc = (begin_square == begin_row) & (pos_row <= pos_square)

    def columns(h):
        return pl.ds(pl.multiple_of(h * HD, HD), HD)

    def copy(kind, i, src, dst, device):
        return pltpu.make_async_remote_copy(
            src_ref=src, dst_ref=dst, send_sem=send_sems.at[kind, i],
            recv_sem=recv_sems.at[kind, i], device_id={"seq": device},
            device_id_type=pl.DeviceIdType.MESH)

    def part(i):
        return pl.ds(i * CHUNK, CHUNK)

    def minor_copy(i):
        return copy(MINOR, i, states.at[minor, part(i)], minor_in.at[part(i)], partner)

    def across_copy(i):
        return copy(ACROSS, i, sum_out.at[part(i)], sum_in.at[part(i)], across)

    def next_copy(i):
        return copy(NEXT, i, total_out.at[part(i)], next_in.at[part(i)], me + 4 * step)

    def second_copy(i):
        return copy(SECOND, i, next_in.at[part(i)], second_in.at[part(i)], me + 4 * step)

    def carry_copy(i):
        return copy(CARRY, i, carry_out.at[part(i)], entering.at[major, part(i)], partner)

    def each(i):
        for j in range(CHUNK):
            h = i * CHUNK + j
            yield h, columns(h)

    def head_states(i):
        for h, at in each(i):
            sg = (g_ref[:, at].astype(F32) * inv_root).astype(BF16)
            sg_ref[:, at] = sg
            states[BACKWARD, h] = dot(q_ref[:, at] * head_rows, sg, (0, 0)).astype(BF16)

    def tail_states(i):
        for h, at in each(i):
            states[FORWARD, h] = dot(k_ref[:, at] * tail_rows, v_ref[:, at], (0, 0)).astype(BF16)

    def scores(i):
        for h, at in each(i):
            w = dot(q_ref[:, at], k_ref[:, at], (1, 1))
            weights_ref[h] = jnp.where(same_doc, w, 0.0).astype(BF16)
            dw = dot(sg_ref[:, at], v_ref[:, at], (1, 1))
            dweights_ref[h] = jnp.where(same_doc, dw, 0.0).astype(BF16)

    def chip_sum(i):
        minor_copy(i).wait_recv()
        for h, _ in each(i):
            sum_out[h] = (states[major, h].astype(F32) + pick(own_clear, minor_in[h])).astype(BF16)

        @pl.when(sends_across)
        def _():
            across_copy(i).start()

    def total(i):
        @pl.when(takes_across)
        def _():
            across_copy(i).wait_recv()

        @pl.when(has_after)
        def _():
            for h, _ in each(i):
                total_out[h] = (pick(is_down | down_clear, sum_out[h])
                                + pick(jnp.logical_not(is_down) | down_clear, sum_in[h])).astype(BF16)

            @pl.when(jnp.logical_not(merges))
            def _():
                next_copy(i).start()

    def relay(i):
        @pl.when(has_before)
        def _():
            next_copy(i).wait_recv()

        @pl.when(merges)
        def _():
            for h, _ in each(i):
                total_out[h] = (total_out[h].astype(F32) + pick(plane_clear, next_in[h])).astype(BF16)
            next_copy(i).start()

    def pass_on(i):
        @pl.when(relays)
        def _():
            second_copy(i).start()

    def enter(i):
        @pl.when(has_second)
        def _():
            second_copy(i).wait_recv()

        for h, _ in each(i):
            carry = pick(is_down, sum_in[h]) + pick(use_next, next_in[h]) + pick(use_second, second_in[h])
            carry_out[h] = carry.astype(BF16)
            entering[major, h] = (minor_in[h].astype(F32) + pick(partner_clear, carry)).astype(BF16)
        carry_copy(i).start()

    def finish_forward(i):
        for h, at in each(i):
            q, sg, state = q_ref[:, at], sg_ref[:, at], entering[FORWARD, h]
            attended = dot(weights_ref[h], v_ref[:, at]) + dot(q * prefix_rows, state)
            attn_ref[:, at] = (attended * inv_root).astype(BF16)
            gq_ref[:, at] = (dot(dweights_ref[h], k_ref[:, at])
                             + dot(sg * prefix_rows, state, (1, 1))).astype(BF16)

    def finish_backward(i):
        for h, at in each(i):
            k, v, state = k_ref[:, at], v_ref[:, at], entering[BACKWARD, h]
            gk_ref[:, at] = (dot(dweights_ref[h], q_ref[:, at], (0, 0))
                             + dot(v * suffix_rows, state, (1, 1))).astype(BF16)
            gv_ref[:, at] = (dot(weights_ref[h], sg_ref[:, at], (0, 0))
                             + dot(k * suffix_rows, state)).astype(BF16)

    def finish_major(i):
        @pl.when(core == 0)
        def _():
            finish_backward(i)

        @pl.when(core == 1)
        def _():
            finish_forward(i)

    def finish_minor(i):
        carry_copy(i).wait_recv()

        @pl.when(core == 0)
        def _():
            finish_forward(i)

        @pl.when(core == 1)
        def _():
            finish_backward(i)

    def at_lag(now, lag, stage, only=True):
        @pl.when((now >= lag) & (now < chunks + lag) & only)
        def _():
            stage(now - lag)

    loads[1].wait()
    loads[2].wait()
    head_states(0)
    peers = jnp.int32(2)
    for by in (-1, 1):
        peers = peers + jnp.where(inside(plane + by), 1, 0)
    pl.semaphore_wait(barrier, peers)

    @pl.when(core == 1)
    def _():
        minor_copy(0).start()

    @pl.loop(1, chunks + 2)
    def _(i):
        @pl.when(i < chunks)
        def _():
            head_states(i)

            @pl.when(core == 1)
            def _():
                minor_copy(i).start()
        at_lag(i, 2, chip_sum, core == 0)

    loads[3].wait()
    loads[4].wait()

    @pl.loop(0, chunks + 4)
    def _(i):
        @pl.when(i < chunks)
        def _():
            tail_states(i)

            @pl.when(core == 0)
            def _():
                minor_copy(i).start()
        at_lag(i, 0, scores, core == 1)
        at_lag(i, 4, chip_sum, core == 1)

    enter_lag = jnp.where(has_second, 5, 3)
    minor_lag = jnp.where(core == 0, 7, 5)

    @pl.loop(0, chunks + 7)
    def _(i):
        at_lag(i, 0, scores, core == 0)
        at_lag(i, 0, total)
        at_lag(i, 2, relay)
        at_lag(i, 2, pass_on)
        at_lag(i, enter_lag, enter)
        at_lag(i, enter_lag, finish_major)
        at_lag(i, minor_lag, finish_minor)

    @pl.loop(0, chunks)
    def _(i):
        minor_copy(i).wait_send()
        carry_copy(i).wait_send()

        @pl.when(sends_across)
        def _():
            across_copy(i).wait_send()

        @pl.when(has_after)
        def _():
            next_copy(i).wait_send()

        @pl.when(relays)
        def _():
            second_copy(i).wait_send()


def place(*refs):
    sources, targets, sems = refs[:4], refs[4:8], refs[8]
    moves = [pltpu.make_async_copy(src, dst, sems.at[i]) for i, (src, dst) in enumerate(zip(sources, targets))]
    for move in moves:
        move.start()
    for move in moves:
        move.wait()


def per_device(n, queries, keys, values, grad_out, doc_lengths):
    rows, width = queries.shape
    heads = width // HD
    chunks = heads // CHUNK
    remote = pl.BlockSpec(memory_space=pltpu.HBM)
    local = pl.BlockSpec(memory_space=pltpu.VMEM)
    held = pltpu.VMEM((rows, width), BF16)
    state = pltpu.VMEM((heads, HD, HD), BF16)
    pair = pltpu.VMEM((2, heads, HD, HD), BF16)
    square = pltpu.VMEM((heads, rows, rows), BF16)
    out = jax.ShapeDtypeStruct((rows, width), BF16)
    outputs_bytes = 4 * rows * width * 2
    results = pl.pallas_call(
        functools.partial(kernel, n, doc_lengths.shape[0], heads),
        out_shape=(held,) * 4,
        in_specs=[remote] * 5,
        out_specs=(local,) * 4,
        scratch_shapes=[pltpu.SMEM(doc_lengths.shape, jnp.int32)] + [held] * 4
        + [pltpu.SemaphoreType.DMA((5,)), held, pair] + [state] * 7 + [pair, square, square]
        + [pltpu.SemaphoreType.DMA((5, chunks))] * 2,
        compiler_params=pltpu.CompilerParams(
            collective_id=0, has_side_effects=True, vmem_limit_bytes=VMEM_BYTES - outputs_bytes),
    )(doc_lengths, queries, keys, values, grad_out)
    return pl.pallas_call(
        place,
        out_shape=(out,) * 4,
        in_specs=[local] * 4,
        out_specs=(remote,) * 4,
        scratch_shapes=[pltpu.SemaphoreType.DMA((4,))],
        compiler_params=pltpu.CompilerParams(vmem_limit_bytes=16_000_000),
    )(*results)


def solution(mesh):
    rows = P(("groups", "seq"), None)
    return jax.shard_map(
        functools.partial(per_device, mesh.shape["seq"]),
        mesh=mesh,
        in_specs=(rows, rows, rows, rows, P("groups")),
        out_specs=(rows,) * 4,
        check_vma=False,
    )
```

time: 30.2 us -> 29.2 us (0.967)
  Pallas kernels: 29.4 us -> 28.4 us
    pallas_call x1, Pallas kernels: 28.1 us -> 27 us  [per_device(): pl.pallas_call(functools.partial(kernel, n, doc_lengths.shape[0], heads),...]
where the time goes in v2:
time: 29.2 us; the launch traced here: 29 us
  Pallas kernels  28.4 us (97%)
  between operations  0.64 us (2%)
    pallas_call x1, Pallas kernels, per_device(): pl.pallas_call(functools.partial(kernel, n, doc_lengths.shape[0], heads),...  27 us
    pallas_call x1, Pallas kernels, per_device(): pl.pallas_call(place, out_shape=(out,) * 4, in_specs=[local] * 4, out_spe...  1.35 us

profile of v2, /device:TPU:1, one launch (start us, length us, event | category | flops | bytes accessed | tf_op | source)
XLA Modules:
  0.0 29.0 jit_solution(17287498985485471322)
XLA Ops:
  0.6 27.0 %shard_map.84 = (bf16[128,2048]{1,0:T(8,128)(2,1)S(1)}, bf16[128,2048]{1,0:T(8,128)(2,1)S(1)}, bf16[128,2048]{1,0:T(8,128)(2,1)S(1)}, bf16[128,2048]{1,0:T(8,128)(2,1)S(1)}) custom-call(s32[8]{0:T(128)} %lengths_hbm.1, bf16[128,2048]{1,0:T(8,128)(2,1)} %q_hbm.1, bf16[128,2048]{1,0:T(8,128)(2,1)} %k_hbm.1, bf16[128,2048]{1,0:T(8,128)(2,1)} %v_hbm.1, ...), custom_call_target="tpu_custom_call" | custom-call | tf_op jit(solution)/shard_map/pallas_call | solution.py:354
  27.7 1.3 %shard_map.85 = (bf16[128,2048]{1,0:T(8,128)(2,1)}, bf16[128,2048]{1,0:T(8,128)(2,1)}, bf16[128,2048]{1,0:T(8,128)(2,1)}, bf16[128,2048]{1,0:T(8,128)(2,1)}) custom-call(bf16[128,2048]{1,0:T(8,128)(2,1)S(1)} %get-tuple-element.8.refs_0_, bf16[128,2048]{1,0:T(8,128)(2,1)S(1)} %get-tuple-element.9.refs_1_, bf16[128,2048]{1,0:T(8,128)(2,1)S(1)} %get-tuple-element.10.refs_2_, ...), custom_call_target="tpu_custom_call" | custom-call | tf_op jit(solution)/shard_map/pallas_call | solution.py:365
